TPU v7x, 32 devices: a whole 2x2x4 slice. The times are simulated.
32 devices in a mesh: heads: 4 (over z), rows: 8 (over y, x, core).
Axes of the slice: x: 2, y: 2, z: 4, core: 2. Of those that a mesh axis runs over, the one named last changes fastest.
Arguments:
- tokens: bfloat16 [4, 2048, 1024], P(None, 'rows'), may hold values from -6 to 6
- cam_index: int32 [4, 2048], P(None, 'rows'), may hold values from 0 to 31
- patches: bfloat16 [4, 2048, 768], P(None, 'rows'), may hold values from -6 to 6
- patch_len: int32 [4], replicated, may hold values from 512 to 2048, as said below
- camera_table: bfloat16 [32, 2, 1024], replicated, may hold values from -3 to 3
- self_weights: bfloat16 [3, 1024, 1024], P(None, None, 'heads'), may hold values from -0.1875 to 0.1875
- self_output: bfloat16 [1024, 1024], P('heads'), may hold values from -4 to 4
- cross_gain: bfloat16 [1024], replicated, may hold values from 0.5 to 1.5
- cross_query: bfloat16 [1024, 1024], P(None, 'heads'), may hold values from -0.1875 to 0.1875
- cross_pair: bfloat16 [2, 1024, 1024], P(None, None, 'heads'), may hold values from -0.1875 to 0.1875
- cross_output: bfloat16 [1024, 1024], P('heads'), may hold values from -4 to 4
- patch_weights: bfloat16 [768, 1024], replicated, may hold values from -0.21875 to 0.21875
- hidden_gain: bfloat16 [1024], replicated, may hold values from 0.5 to 1.5
- widen_weights: bfloat16 [1024, 4096], P(None, 'heads'), may hold values from -0.1875 to 0.1875
- narrow_weights: bfloat16 [4096, 1024], P('heads'), may hold values from -0.09375 to 0.09375
- cotangent: bfloat16 [4, 2048, 1024], P(None, 'rows'), may hold values from -6 to 6
Outputs:
- tokens_out: bfloat16 [4, 2048, 1024], P(None, 'rows')
- input_grad: float32 [4, 2048, 1024], P(None, 'rows')
- patch_grad: float32 [4, 2048, 768], P(None, 'rows')
- grad_camera_table: float32 [32, 2, 1024], P(None, None, 'heads')
- grad_self_weights: float32 [3, 1024, 1024], P(None, None, 'heads')
- grad_self_output: float32 [1024, 1024], P('heads')
- grad_cross_gain: float32 [1024], P('heads')
- grad_cross_query: float32 [1024, 1024], P(None, 'heads')
- grad_cross_pair: float32 [2, 1024, 1024], P(None, None, 'heads')
- grad_cross_output: float32 [1024, 1024], P('heads')
- grad_patch_weights: float32 [768, 1024], P(None, 'heads')
- grad_hidden_gain: float32 [1024], P('heads')
- grad_widen_weights: float32 [1024, 4096], P(None, 'heads')
- grad_narrow_weights: float32 [4096, 1024], P('heads')
Inputs may be any that keep to these rules, and one draw needn't show every extreme that they name: `patch_len`: each entry is 2048 or a quarter of 2048; both values occur in every draw. Live patch tokens are the first ones of the object.
All inputs are finite; a program needn't handle non-finite values.
Results may differ from a plain program's by a relative error of at most 0.028.
The roundings to bfloat16 on the way count: a program that leaves them out, or rounds other values in their place, can miss the bound.
Values may be sent and summed in bfloat16 or wider, within the bound.
No kernel may reach another device: no remote copies, remote signals or barrier semaphores. Data moves between devices by JAX's collectives and lax.ppermute only.
A program may use at most 448 MiB of HBM per device.

v0:
```python
from functools import reduce
import jax
import jax.numpy as jnp
from jax import lax
from jax.sharding import PartitionSpec as P

HEAD_DIM = 64
EPSILON = 1e-05


def layer_norm(inputs):
    centred = inputs - jnp.mean(inputs, axis=-1, keepdims=True)
    return centred * lax.rsqrt(jnp.mean(centred * centred, axis=-1, keepdims=True) + EPSILON)


def modulated(inputs, shift_scale):
    return layer_norm(inputs) * (1.0 + shift_scale[:, 0]) + shift_scale[:, 1]


def gained(inputs, gain_row):
    return layer_norm(inputs) * gain_row


def gelu_tanh(pre_act):
    return jax.nn.gelu(pre_act, approximate=True)


def by_heads(matrix):
    return matrix.reshape(matrix.shape[0], -1, HEAD_DIM)


def scaled_scores(queries, key_rows):
    return jnp.einsum(
        "qhe,khe->hqk", queries, key_rows, preferred_element_type=jnp.float32
    ) * HEAD_DIM ** (-0.5)


def attend_forward(queries, key_rows, value_rows, mask_add):
    scores = scaled_scores(queries, key_rows) + mask_add
    row_peak = jnp.max(scores, axis=-1, keepdims=True)
    raised = jnp.exp(scores - row_peak)
    row_total = jnp.sum(raised, axis=-1, keepdims=True)
    attn_probs = (raised / row_total).astype(jnp.bfloat16)
    mixed_out = jnp.einsum(
        "hqk,khe->qhe", attn_probs, value_rows, preferred_element_type=jnp.float32
    )
    return (mixed_out.reshape(mixed_out.shape[0], -1).astype(jnp.bfloat16), row_peak, row_total)


def attend_queries_back(queries, key_rows, value_rows, mask_add, row_peak, row_total, grad_mixed):
    score_scale = HEAD_DIM ** (-0.5)
    scores = scaled_scores(queries, key_rows) + mask_add
    attn_probs = jnp.exp(scores - row_peak) / row_total
    grad_probs = jnp.einsum(
        "qhe,khe->hqk", grad_mixed, value_rows, preferred_element_type=jnp.float32
    )
    spread = jnp.sum(attn_probs * grad_probs, axis=-1, keepdims=True)
    grad_scores = (attn_probs * (grad_probs - spread)).astype(jnp.bfloat16)
    grad_queries = (
        jnp.einsum("hqk,khe->qhe", grad_scores, key_rows, preferred_element_type=jnp.float32)
        * score_scale
    )
    return (grad_queries, spread)


def attend_keys_back(
    all_queries, key_rows, value_rows, mask_add, all_peak, all_total, all_spread, all_grad
):
    score_scale = HEAD_DIM ** (-0.5)
    scores = scaled_scores(all_queries, key_rows) + mask_add
    attn_probs = jnp.exp(scores - all_peak) / all_total
    grad_probs = jnp.einsum(
        "qhe,khe->hqk", all_grad, value_rows, preferred_element_type=jnp.float32
    )
    grad_scores = (attn_probs * (grad_probs - all_spread)).astype(jnp.bfloat16)
    grad_keys = (
        jnp.einsum("hqk,qhe->khe", grad_scores, all_queries, preferred_element_type=jnp.float32)
        * score_scale
    )
    grad_values = jnp.einsum(
        "hqk,qhe->khe",
        attn_probs.astype(jnp.bfloat16),
        all_grad,
        preferred_element_type=jnp.float32,
    )
    return (grad_keys, grad_values)


def owner_key_grads(
    queries, grad_mixed, row_peak, row_total, spread, own_keys, own_values, own_mask
):
    gathered_queries, gathered_grads = (
        lax.all_gather(queries, "rows", axis=0, tiled=True),
        lax.all_gather(grad_mixed, "rows", axis=0, tiled=True),
    )
    gathered_peak, gathered_total, gathered_spread = (
        lax.all_gather(row_peak[:, :, 0].T, "rows", axis=0, tiled=True),
        lax.all_gather(row_total[:, :, 0].T, "rows", axis=0, tiled=True),
        lax.all_gather(spread[:, :, 0].T, "rows", axis=0, tiled=True),
    )
    grad_keys, grad_values = attend_keys_back(
        by_heads(gathered_queries),
        by_heads(own_keys),
        by_heads(own_values),
        own_mask,
        gathered_peak.T[:, :, None],
        gathered_total.T[:, :, None],
        gathered_spread.T[:, :, None],
        by_heads(gathered_grads),
    )
    return (grad_keys.reshape(own_keys.shape[0], -1), grad_values.reshape(own_keys.shape[0], -1))


def add_trees(former, latter):
    return jax.tree.map(jnp.add, former, latter)


def per_device(
    tokens,
    cam_index,
    patches,
    patch_len,
    camera_table,
    self_weights,
    self_output,
    cross_gain,
    cross_query,
    cross_pair,
    cross_output,
    patch_weights,
    hidden_gain,
    widen_weights,
    narrow_weights,
    cotangent,
):
    batches = tokens.shape[0]
    row_count = tokens.shape[1]
    model_width = tokens.shape[2]
    local_cols = self_weights.shape[2]
    code_count = camera_table.shape[0]
    patch_rows = patches.shape[1]
    row_rank = lax.axis_index("rows")
    head_rank = lax.axis_index("heads")
    all_patches = patch_rows * lax.axis_size("rows")
    table_flat = camera_table.reshape(code_count, -1).astype(jnp.float32)
    patch_index = jnp.arange(all_patches)
    own_index = row_rank * patch_rows + jnp.arange(patch_rows)
    cross_gain_f = cross_gain.astype(jnp.float32)
    hidden_gain_f = hidden_gain.astype(jnp.float32)
    outputs = []
    input_grads = []
    patch_grads = []
    contributions = []
    for microbatch in range(batches):
        inputs = tokens[microbatch].astype(jnp.float32)
        onehot = (cam_index[microbatch][:, None] == jnp.arange(code_count)[None, :]).astype(
            jnp.float32
        )
        shift_scale = jnp.dot(onehot, table_flat, precision=lax.Precision.HIGHEST).reshape(
            row_count, 2, model_width
        )
        normed_one, norm_one_back = jax.vjp(modulated, inputs, shift_scale)
        normed_one_low = normed_one.astype(jnp.bfloat16)
        projected = jnp.einsum(
            "rd,tdc->trc", normed_one_low, self_weights, preferred_element_type=jnp.float32
        ).astype(jnp.bfloat16)
        queries = projected[0]
        all_keys, all_values = (
            lax.all_gather(projected[1], "rows", axis=0, tiled=True),
            lax.all_gather(projected[2], "rows", axis=0, tiled=True),
        )
        self_mixed, self_peak, self_total = attend_forward(
            by_heads(queries), by_heads(all_keys), by_heads(all_values), 0.0
        )
        attn_sum = lax.psum(
            jnp.dot(self_mixed, self_output, preferred_element_type=jnp.float32), "heads"
        )
        after_self = inputs + attn_sum
        normed_two, norm_two_back = jax.vjp(gained, after_self, cross_gain_f)
        normed_two_low = normed_two.astype(jnp.bfloat16)
        cross_queries = jnp.dot(
            normed_two_low, cross_query, preferred_element_type=jnp.float32
        ).astype(jnp.bfloat16)
        patch_mid = jnp.dot(
            patches[microbatch], patch_weights, preferred_element_type=jnp.float32
        ).astype(jnp.bfloat16)
        patch_pair = jnp.einsum(
            "pd,tdc->tpc", patch_mid, cross_pair, preferred_element_type=jnp.float32
        ).astype(jnp.bfloat16)
        own_keys = patch_pair[0]
        own_values = patch_pair[1]
        cross_keys_all, cross_values_all = (
            lax.all_gather(own_keys, "rows", axis=0, tiled=True),
            lax.all_gather(own_values, "rows", axis=0, tiled=True),
        )
        mask_add = jnp.where(patch_index < patch_len[microbatch], 0.0, -1e30).astype(jnp.float32)
        cross_mixed, cross_peak, cross_total = attend_forward(
            by_heads(cross_queries), by_heads(cross_keys_all), by_heads(cross_values_all), mask_add
        )
        cross_sum = lax.psum(
            jnp.dot(cross_mixed, cross_output, preferred_element_type=jnp.float32).astype(
                jnp.bfloat16
            ),
            "heads",
        ).astype(jnp.float32)
        after_cross = after_self + cross_sum
        normed_three, norm_three_back = jax.vjp(gained, after_cross, hidden_gain_f)
        normed_three_low = normed_three.astype(jnp.bfloat16)
        pre_act = jnp.dot(normed_three_low, widen_weights, preferred_element_type=jnp.float32)
        activated, act_back = jax.vjp(gelu_tanh, pre_act)
        activated_low = activated.astype(jnp.bfloat16)
        hidden_sum = lax.psum(
            jnp.dot(activated_low, narrow_weights, preferred_element_type=jnp.float32).astype(
                jnp.bfloat16
            ),
            "heads",
        ).astype(jnp.float32)
        outputs.append((after_cross + hidden_sum).astype(jnp.bfloat16))
        grad_low = cotangent[microbatch]
        grad_top = grad_low.astype(jnp.float32)
        narrow_term = jnp.einsum(
            "rf,rd->fd", activated_low, grad_low, preferred_element_type=jnp.float32
        )
        grad_act = jnp.einsum(
            "rd,fd->rf", grad_low, narrow_weights, preferred_element_type=jnp.float32
        )
        grad_pre = act_back(grad_act)[0].astype(jnp.bfloat16)
        widen_term = jnp.einsum(
            "rd,rf->df", normed_three_low, grad_pre, preferred_element_type=jnp.float32
        )
        grad_normed_three = lax.psum(
            jnp.einsum(
                "rf,df->rd", grad_pre, widen_weights, preferred_element_type=jnp.float32
            ).astype(jnp.bfloat16),
            "heads",
        ).astype(jnp.float32)
        grad_mid, hidden_gain_term = norm_three_back(grad_normed_three)
        grad_cross = grad_top + grad_mid
        grad_cross_low = grad_cross.astype(jnp.bfloat16)
        cross_output_term = jnp.einsum(
            "rc,rd->cd", cross_mixed, grad_cross_low, preferred_element_type=jnp.float32
        )
        grad_cross_mixed = jnp.einsum(
            "rd,cd->rc", grad_cross_low, cross_output, preferred_element_type=jnp.float32
        ).astype(jnp.bfloat16)
        grad_cq, cross_spread = attend_queries_back(
            by_heads(cross_queries),
            by_heads(cross_keys_all),
            by_heads(cross_values_all),
            mask_add,
            cross_peak,
            cross_total,
            by_heads(grad_cross_mixed),
        )
        own_mask = jnp.where(own_index < patch_len[microbatch], 0.0, -1e30).astype(jnp.float32)
        grad_ck, grad_cv = owner_key_grads(
            cross_queries,
            grad_cross_mixed,
            cross_peak,
            cross_total,
            cross_spread,
            own_keys,
            own_values,
            own_mask,
        )
        grad_pair_low = jnp.stack([grad_ck, grad_cv]).astype(jnp.bfloat16)
        pair_term = jnp.einsum(
            "pd,tpc->tdc", patch_mid, grad_pair_low, preferred_element_type=jnp.float32
        )
        grad_cq_low = grad_cq.reshape(row_count, -1).astype(jnp.bfloat16)
        query_term = jnp.einsum(
            "rd,rc->dc", normed_two_low, grad_cq_low, preferred_element_type=jnp.float32
        )
        grad_normed_two, grad_patch_mid = (
            lax.psum(
                jnp.einsum(
                    "rc,dc->rd", grad_cq_low, cross_query, preferred_element_type=jnp.float32
                ).astype(jnp.bfloat16),
                "heads",
            ).astype(jnp.float32),
            lax.psum(
                jnp.einsum(
                    "tpc,tdc->pd", grad_pair_low, cross_pair, preferred_element_type=jnp.float32
                ).astype(jnp.bfloat16),
                "heads",
            ).astype(jnp.float32),
        )
        grad_mid_low = grad_patch_mid.astype(jnp.bfloat16)
        own_columns = lax.dynamic_slice_in_dim(grad_mid_low, head_rank * local_cols, local_cols, 1)
        patch_term = jnp.einsum(
            "pe,pc->ec", patches[microbatch], own_columns, preferred_element_type=jnp.float32
        )
        patch_grads.append(
            jnp.einsum("pd,ed->pe", grad_mid_low, patch_weights, preferred_element_type=jnp.float32)
        )
        grad_after_self, cross_gain_term = norm_two_back(grad_normed_two)
        grad_self = grad_cross + grad_after_self
        grad_self_low = grad_self.astype(jnp.bfloat16)
        self_output_term = jnp.einsum(
            "rc,rd->cd", self_mixed, grad_self_low, preferred_element_type=jnp.float32
        )
        grad_self_mixed = jnp.einsum(
            "rd,cd->rc", grad_self_low, self_output, preferred_element_type=jnp.float32
        ).astype(jnp.bfloat16)
        grad_q, self_spread = attend_queries_back(
            by_heads(queries),
            by_heads(all_keys),
            by_heads(all_values),
            0.0,
            self_peak,
            self_total,
            by_heads(grad_self_mixed),
        )
        grad_k, grad_v = owner_key_grads(
            queries,
            grad_self_mixed,
            self_peak,
            self_total,
            self_spread,
            projected[1],
            projected[2],
            0.0,
        )
        grad_proj = jnp.stack([grad_q.reshape(row_count, -1), grad_k, grad_v]).astype(jnp.bfloat16)
        self_term = jnp.einsum(
            "rd,trc->tdc", normed_one_low, grad_proj, preferred_element_type=jnp.float32
        )
        grad_normed_one = lax.psum(
            jnp.einsum(
                "trc,tdc->rd", grad_proj, self_weights, preferred_element_type=jnp.float32
            ).astype(jnp.bfloat16),
            "heads",
        ).astype(jnp.float32)
        grad_inputs, grad_shift_scale = norm_one_back(grad_normed_one)
        table_term = jnp.dot(
            onehot.T, grad_shift_scale.reshape(row_count, -1), precision=lax.Precision.HIGHEST
        )
        input_grads.append(grad_self + grad_inputs)
        contributions.append(
            (
                table_term,
                self_term,
                self_output_term,
                cross_gain_term,
                query_term,
                pair_term,
                cross_output_term,
                patch_term,
                hidden_gain_term,
                widen_term,
                narrow_term,
            )
        )
    summed = reduce(add_trees, contributions)
    table_part = lax.dynamic_slice_in_dim(
        summed[0].reshape(code_count, 2, model_width), head_rank * local_cols, local_cols, 2
    )
    cross_gain_part = lax.dynamic_slice_in_dim(summed[3], head_rank * local_cols, local_cols, 0)
    hidden_gain_part = lax.dynamic_slice_in_dim(summed[8], head_rank * local_cols, local_cols, 0)
    totals = (
        lax.psum(table_part.astype(jnp.bfloat16), "rows").astype(jnp.float32),
        lax.psum(summed[1].astype(jnp.bfloat16), "rows").astype(jnp.float32),
        lax.psum(summed[2].astype(jnp.bfloat16), "rows").astype(jnp.float32),
        lax.psum(cross_gain_part.astype(jnp.bfloat16), "rows").astype(jnp.float32),
        lax.psum(summed[4].astype(jnp.bfloat16), "rows").astype(jnp.float32),
        lax.psum(summed[5].astype(jnp.bfloat16), "rows").astype(jnp.float32),
        lax.psum(summed[6].astype(jnp.bfloat16), "rows").astype(jnp.float32),
        lax.psum(summed[7].astype(jnp.bfloat16), "rows").astype(jnp.float32),
        lax.psum(hidden_gain_part.astype(jnp.bfloat16), "rows").astype(jnp.float32),
        lax.psum(summed[9].astype(jnp.bfloat16), "rows").astype(jnp.float32),
        lax.psum(summed[10].astype(jnp.bfloat16), "rows").astype(jnp.float32),
    )
    return (jnp.stack(outputs), jnp.stack(input_grads), jnp.stack(patch_grads)) + tuple(totals)


def solution(mesh):
    in_specs = (
        P(None, "rows", None),
        P(None, "rows"),
        P(None, "rows", None),
        P(),
        P(),
        P(None, None, "heads"),
        P("heads", None),
        P(),
        P(None, "heads"),
        P(None, None, "heads"),
        P("heads", None),
        P(),
        P(),
        P(None, "heads"),
        P("heads", None),
        P(None, "rows", None),
    )
    out_specs = (
        P(None, "rows", None),
        P(None, "rows", None),
        P(None, "rows", None),
        P(None, None, "heads"),
        P(None, None, "heads"),
        P("heads", None),
        P("heads"),
        P(None, "heads"),
        P(None, None, "heads"),
        P("heads", None),
        P(None, "heads"),
        P("heads"),
        P(None, "heads"),
        P("heads", None),
    )
    return jax.shard_map(
        per_device, mesh=mesh, in_specs=in_specs, out_specs=out_specs, check_vma=False
    )
```

profile of v0, /device:TPU:0, one launch (start us, length us, event | category | flops | bytes accessed | tf_op | source)
XLA Modules:
  0.0 1912.5 jit_solution(12267981073876656317)
XLA Ops:
  53.8 17.8 all-gather.85.cloned.1.call-done
  78.5 19.1 all-gather.103.cloned.1.call-done
  105.1 17.8 all-gather.101.cloned.1.call-done
  128.6 20.3 %all-gather.95.cloned.1.call-done = bf16[1,2048,256]{1,2,0:T(8,128)(2,1)} async-done(((bf16[1,256,256]{1,2,0:T(8,128)(2,1)}), bf16[1,2048,256]{1,2,0:T(8,128)(2,1)}) %all-gather.95.cloned.1.call-update) | async-done | bytes 1048592 | tf_op jit(solution)/shard_map/all_gather | solution.py:169
  156.3 17.9 all-gather.93.cloned.1.call-done
  179.8 19.8 %all-gather.79.cloned.1.call-done = bf16[1,2048,256]{1,2,0:T(8,128)(2,1)} async-done(((bf16[1,256,256]{1,2,0:T(8,128)(2,1)}), bf16[1,2048,256]{1,2,0:T(8,128)(2,1)}) %all-gather.79.cloned.1.call-update) | async-done | bytes 1048592 | tf_op jit(solution)/shard_map/all_gather | solution.py:169
  210.0 15.2 all-gather.77.cloned.1.call-done
  349.1 112.7 %all-reduce.22.cloned.1.call-done = (f32[256,1024]{1,0:T(8,128)}, f32[256,1024]{1,0:T(8,128)}, f32[256,1024]{1,0:T(8,128)}, f32[256,1024]{1,0:T(8,128)}) async-done(((f32[256,1024]{1,0:T(8,128)}, f32[256,1024]{1,0:T(8,128)}, f32[256,1024]{1,0:T(8,128)}, f32[256,1024]{1,0:T(8,128)}), (f32[256,1024]{1,0:T(8,128)}, f32[256,1024]{1,0:T(8,128)}, f32[256,1024]{1,0:T(8,128)}, ...) | async-done | bytes 4194320 | tf_op jit(solution)/shard_map/psum | solution.py:175
  469.0 17.5 all-gather.115.cloned.1.call-done
  494.1 17.8 all-gather.107.cloned.1.call-done
  516.7 10.0 all_gather.221
  547.5 15.5 all-gather.89.cloned.1.call-done
  568.9 19.6 %all-gather.83.cloned.1.call-done = bf16[1,2048,256]{1,2,0:T(8,128)(2,1)} async-done(((bf16[1,256,256]{1,2,0:T(8,128)(2,1)}), bf16[1,2048,256]{1,2,0:T(8,128)(2,1)}) %all-gather.83.cloned.1.call-update) | async-done | bytes 1048592 | tf_op jit(solution)/shard_map/all_gather | solution.py:193
  596.9 17.1 all-gather.81.cloned.1.call-done
  619.9 19.8 %all-gather.99.cloned.1.call-done = bf16[1,2048,256]{1,2,0:T(8,128)(2,1)} async-done(((bf16[1,256,256]{1,2,0:T(8,128)(2,1)}), bf16[1,2048,256]{1,2,0:T(8,128)(2,1)}) %all-gather.99.cloned.1.call-update) | async-done | bytes 1048592 | tf_op jit(solution)/shard_map/all_gather | solution.py:193
  647.5 10.0 all_gather.216
  666.6 10.4 all_gather.211
  694.2 9.9 all_gather.206
  729.4 12.9 all-gather.69.cloned.1.call-done
  748.4 19.4 %all-gather.65.cloned.1.call-done = bf16[2048,256]{0,1:T(8,128)(2,1)} async-done(((bf16[256,256]{0,1:T(8,128)(2,1)}), bf16[2048,256]{0,1:T(8,128)(2,1)}) %all-gather.65.cloned.1.call-update) | async-done | bytes 1048592 | tf_op jit(solution)/shard_map/all_gather | solution.py:93
  774.0 19.4 %all-gather.61.cloned.1.call-done = bf16[2048,256]{0,1:T(8,128)(2,1)} async-done(((bf16[256,256]{0,1:T(8,128)(2,1)}), bf16[2048,256]{0,1:T(8,128)(2,1)}) %all-gather.61.cloned.1.call-update) | async-done | bytes 1048592 | tf_op jit(solution)/shard_map/all_gather | solution.py:93
  799.6 85.7 %all-reduce.32.cloned.1.call-done = (bf16[256,1024]{1,0:T(8,128)(2,1)}, bf16[256,1024]{1,0:T(8,128)(2,1)}, bf16[256,1024]{1,0:T(8,128)(2,1)}, bf16[256,1024]{1,0:T(8,128)(2,1)}) async-done(((bf16[256,1024]{1,0:T(8,128)(2,1)}, bf16[256,1024]{1,0:T(8,128)(2,1)}, bf16[256,1024]{1,0:T(8,128)(2,1)}, bf16[256,1024]{1,0:T(8,128)(2,1)}), (bf16[256,1024]{1,0:T(8,128)(2,1)}, bf16[256,1024]{1,0:T(8,128)(2,1)}, ...) | async-done | bytes 2097168 | tf_op jit(solution)/shard_map/psum | solution.py:200
  940.0 68.7 %all-reduce.30.cloned.1.call-done = (bf16[256,1024]{1,0:T(8,128)(2,1)}, bf16[256,1024]{1,0:T(8,128)(2,1)}, bf16[256,1024]{1,0:T(8,128)(2,1)}, bf16[256,1024]{1,0:T(8,128)(2,1)}) async-done(((bf16[256,1024]{1,0:T(8,128)(2,1)}, bf16[256,1024]{1,0:T(8,128)(2,1)}, bf16[256,1024]{1,0:T(8,128)(2,1)}, bf16[256,1024]{1,0:T(8,128)(2,1)}), (bf16[256,1024]{1,0:T(8,128)(2,1)}, bf16[256,1024]{1,0:T(8,128)(2,1)}, ...) | async-done | bytes 2097168 | tf_op jit(solution)/shard_map/psum | solution.py:231
  1179.4 61.4 %all-reduce.28.cloned.1.call-done = (bf16[256,1024]{1,0:T(8,128)(2,1)}, bf16[256,1024]{1,0:T(8,128)(2,1)}, bf16[256,1024]{1,0:T(8,128)(2,1)}, bf16[256,1024]{1,0:T(8,128)(2,1)}) async-done(((bf16[256,1024]{1,0:T(8,128)(2,1)}, bf16[256,1024]{1,0:T(8,128)(2,1)}, bf16[256,1024]{1,0:T(8,128)(2,1)}, bf16[256,1024]{1,0:T(8,128)(2,1)}), (bf16[256,1024]{1,0:T(8,128)(2,1)}, bf16[256,1024]{1,0:T(8,128)(2,1)}, ...) | async-done | bytes 2097168 | tf_op jit(solution)/shard_map/psum | solution.py:275
  1272.3 10.3 multiply_reduce_fusion.4
  1335.6 10.7 all_gather.198
  1346.3 9.3 all_gather.193
  1355.6 10.2 all_gather.188
  1365.8 9.3 all_gather.203
  1471.0 204.0 %all-reduce.26.cloned.1.call-done = (bf16[256,1024]{1,0:T(8,128)(2,1)}, bf16[256,1024]{1,0:T(8,128)(2,1)}, bf16[256,1024]{1,0:T(8,128)(2,1)}, bf16[256,1024]{1,0...) async-done(((bf16[256,1024]{1,0:T(8,128)(2,1)}, ...) | async-done | bytes 6291472 | tf_op jit(solution)/shard_map/psum | solution.py:281
  1722.2 24.8 %all-reduce.9 = (bf16[32,2,256]{2,1,0:T(2,128)(2,1)S(1)}, bf16[256]{0:T(256)(128)(2,1)S(1)}, bf16[256]{0:T(256)(128)(2,1)S(1)}) all-reduce(bf16[32,2,256]{2,1,0:T(2,128)(2,1)S(1)} %dynamic-slice_convert_fusion, bf16[256]{0:T(256)(128)(2,1)S(1)} %dynamic_slice.40, ...), channel_id=1, replica_groups=mesh['heads'=4,'rows'=8] {'rows'}, use_global_device_ids=true, to_apply=%region_100.101 | all-reduce | flops 16896 | bytes 67584 | tf_op jit(solution)/shard_map/psum | solution.py:361
  1769.1 116.2 %all-reduce.24.cloned.1.call-done = (bf16[3,1024,256]{1,2,0:T(8,128)(2,1)}, bf16[2,1024,256]{1,2,0:T(8,128)(2,1)}, bf16[768,256]{0,1:T(8,128)(2,1)}, bf16[256,10...) async-done(((bf16[3,1024,256]{1,2,0:T(8,128)(2,1)}, ...) | async-done | bytes 8781840 | tf_op jit(solution)/shard_map/psum | solution.py:362
  (1102 shorter events, 843.2 us)
Async XLA Ops:
  23.4 99.6 %all-gather.101.cloned.1.call-start = ((), (), s32[]{:S(2)}) async-start(), calls=%async_computation.24 | async-start | bytes 1179648 | tf_op jit(solution)/shard_map/all_gather | solution.py:170
  24.0 124.9 %all-gather.95.cloned.1.call-start = ((), (), s32[]{:S(2)}) async-start(), calls=%async_computation.21 | async-start | bytes 1179648 | tf_op jit(solution)/shard_map/all_gather | solution.py:169
  26.9 147.3 %all-gather.93.cloned.1.call-start = ((), (), s32[]{:S(2)}) async-start(), calls=%async_computation.20 | async-start | bytes 1179648 | tf_op jit(solution)/shard_map/all_gather | solution.py:170
  27.5 172.2 %all-gather.79.cloned.1.call-start = ((), (), s32[]{:S(2)}) async-start(), calls=%async_computation.13 | async-start | bytes 1179648 | tf_op jit(solution)/shard_map/all_gather | solution.py:169
  34.0 191.2 %all-gather.77.cloned.1.call-start = ((), (), s32[]{:S(2)}) async-start(), calls=%async_computation.12 | async-start | bytes 1179648 | tf_op jit(solution)/shard_map/all_gather | solution.py:170
  34.7 278.7 %all-gather.113.cloned.1.call-start = ((), (), s32[]{:S(2)}) async-start(), calls=%async_computation.30 | async-start | bytes 1179648 | tf_op jit(solution)/shard_map/all_gather | solution.py:93
  35.4 284.3 %all-gather.111.cloned.1.call-start = ((), (), s32[]{:S(2)}) async-start(), calls=%async_computation.29 | async-start | bytes 1179648 | tf_op jit(solution)/shard_map/all_gather | solution.py:93
  36.0 289.8 %all-gather.109.cloned.1.call-start = ((), (), s32[]{:S(2)}) async-start(), calls=%async_computation.28 | async-start | bytes 1179648 | tf_op jit(solution)/shard_map/all_gather | solution.py:93
  36.8 425.0 %all-reduce.22.cloned.1.call-start = ((), (), s32[]{:S(2)}) async-start(), calls=%async_computation.32 | async-start | bytes 8388608 | tf_op jit(solution)/shard_map/psum | solution.py:175
  232.8 253.7 %all-gather.115.cloned.1.call-start = ((), (), s32[]{:S(2)}) async-start(), calls=%async_computation.31 | async-start | bytes 1179648 | tf_op jit(solution)/shard_map/all_gather | solution.py:93
  233.5 278.5 %all-gather.107.cloned.1.call-start = ((), (), s32[]{:S(2)}) async-start(), calls=%async_computation.27 | async-start | bytes 1179648 | tf_op jit(solution)/shard_map/all_gather | solution.py:193
  237.9 301.8 %all-gather.91.cloned.1.call-start = ((), (), s32[]{:S(2)}) async-start(), calls=%async_computation.19 | async-start | bytes 1179648 | tf_op jit(solution)/shard_map/all_gather | solution.py:193
  242.2 320.9 %all-gather.89.cloned.1.call-start = ((), (), s32[]{:S(2)}) async-start(), calls=%async_computation.18 | async-start | bytes 1179648 | tf_op jit(solution)/shard_map/all_gather | solution.py:194
  242.8 345.8 %all-gather.83.cloned.1.call-start = ((), (), s32[]{:S(2)}) async-start(), calls=%async_computation.15 | async-start | bytes 1179648 | tf_op jit(solution)/shard_map/all_gather | solution.py:193
  247.0 367.0 %all-gather.81.cloned.1.call-start = ((), (), s32[]{:S(2)}) async-start(), calls=%async_computation.14 | async-start | bytes 1179648 | tf_op jit(solution)/shard_map/all_gather | solution.py:194
  247.6 392.0 %all-gather.99.cloned.1.call-start = ((), (), s32[]{:S(2)}) async-start(), calls=%async_computation.23 | async-start | bytes 1179648 | tf_op jit(solution)/shard_map/all_gather | solution.py:193
  251.3 427.8 %all-gather.105.cloned.1.call-start = ((), (), s32[]{:S(2)}) async-start(), calls=%async_computation.26 | async-start | bytes 1179648 | tf_op jit(solution)/shard_map/all_gather | solution.py:194
  251.9 463.5 %all-gather.97.cloned.1.call-start = ((), (), s32[]{:S(2)}) async-start(), calls=%async_computation.22 | async-start | bytes 1179648 | tf_op jit(solution)/shard_map/all_gather | solution.py:194
  252.7 470.6 %all-gather.73.cloned.1.call-start = ((), (), s32[]{:S(2)}) async-start(), calls=%async_computation.10 | async-start | bytes 1179648 | tf_op jit(solution)/shard_map/all_gather | solution.py:93
  468.9 273.4 %all-gather.69.cloned.1.call-start = ((), (), s32[]{:S(2)}) async-start(), calls=%async_computation.8 | async-start | bytes 1179648 | tf_op jit(solution)/shard_map/all_gather | solution.py:93
  494.1 273.7 %all-gather.65.cloned.1.call-start = ((), (), s32[]{:S(2)}) async-start(), calls=%async_computation.6 | async-start | bytes 1179648 | tf_op jit(solution)/shard_map/all_gather | solution.py:93
  539.4 254.0 %all-gather.61.cloned.1.call-start = ((), (), s32[]{:S(2)}) async-start(), calls=%async_computation.4 | async-start | bytes 1179648 | tf_op jit(solution)/shard_map/all_gather | solution.py:93
  685.1 200.2 %all-reduce.32.cloned.1.call-start = ((), (), s32[]{:S(2)}) async-start(), calls=%async_computation.37 | async-start | bytes 4194304 | tf_op jit(solution)/shard_map/psum | solution.py:200
  723.2 285.5 %all-reduce.30.cloned.1.call-start = ((), (), s32[]{:S(2)}) async-start(), calls=%async_computation.36 | async-start | bytes 4194304 | tf_op jit(solution)/shard_map/psum | solution.py:231
  921.5 200.4 %all-gather.75.cloned.1.call-start = ((), (), s32[]{:S(2)}) async-start(), calls=%async_computation.11 | async-start | bytes 1179648 | tf_op jit(solution)/shard_map/all_gather | solution.py:94
  1111.5 129.3 %all-reduce.28.cloned.1.call-start = ((), (), s32[]{:S(2)}) async-start(), calls=%async_computation.35 | async-start | bytes 4194304 | tf_op jit(solution)/shard_map/psum | solution.py:275
  1121.9 253.6 %all-gather.57.cloned.1.call-start = ((), (), s32[]{:S(2)}) async-start(), calls=%async_computation.2 | async-start | bytes 1179648 | tf_op jit(solution)/shard_map/all_gather | solution.py:94
  1258.2 132.9 %all-gather.55.cloned.1.call-start = ((), (), s32[]{:S(2)}) async-start(), calls=%async_computation.1 | async-start | bytes 1179648 | tf_op jit(solution)/shard_map/all_gather | solution.py:94
  1272.2 134.5 %all-gather.53.cloned.1.call-start = ((), (), s32[]{:S(2)}) async-start(), calls=%async_computation | async-start | bytes 1179648 | tf_op jit(solution)/shard_map/all_gather | solution.py:94
  1291.0 131.4 %all-gather.59.cloned.1.call-start = ((), (), s32[]{:S(2)}) async-start(), calls=%async_computation.3 | async-start | bytes 1179648 | tf_op jit(solution)/shard_map/all_gather | solution.py:94
  1375.2 299.8 %all-reduce.26.cloned.1.call-start = ((), (), s32[]{:S(2)}) async-start(), calls=%async_computation.34 | async-start | bytes 12582912 | tf_op jit(solution)/shard_map/psum | solution.py:281
  1449.2 436.1 %all-reduce.24.cloned.1.call-start = ((), (), s32[]{:S(2)}) async-start(), calls=%async_computation.33 | async-start | bytes 17563648 | tf_op jit(solution)/shard_map/psum | solution.py:362
  (341 other events, 10096.7 us)
Sparse Core Ops, SparseCore 0:
  19.8 26.2 all-gather.86
  47.9 23.5 all-gather.84
  74.0 23.5 all-gather.102
  99.3 23.5 all-gather.100
  125.2 23.5 all-gather.94
  150.6 23.5 all-gather.92
  176.1 23.5 all-gather.78
  201.5 23.5 all-gather.76
  227.6 23.5 all-gather.112
  252.9 23.6 all-gather.110
  278.5 23.6 all-gather.108
  305.7 156.0 all-reduce.21
  488.4 23.5 all-gather.106
  513.9 23.6 all-gather.90
  539.4 23.5 all-gather.88
  564.9 23.5 all-gather.82
  590.4 23.5 all-gather.80
  616.0 23.5 all-gather.98
  641.5 23.7 all-gather.104
  667.3 23.5 all-gather.96
  693.0 23.6 all-gather.72
  718.7 23.5 all-gather.68
  769.8 23.5 all-gather.60
  797.2 88.0 all-reduce.31
  921.6 86.9 all-reduce.29
  1100.1 23.6 all-gather.66
  1126.3 23.5 all-gather.62
  1152.7 87.9 all-reduce.27
  1282.7 23.5 all-gather.54
  1308.8 23.6 all-gather.52
  1449.3 225.6 all-reduce.25
  1754.9 130.3 all-reduce.23
  (6 shorter events, 134.7 us)
where the time goes:
time: 1920 us; the launch traced here: 1910 us
  waiting for transfers between devices  953 us (50%)
  matrix products  489 us (25%)
  blocking collectives  245 us (13%)
  other arithmetic  120 us (6%)
  local copies, waits for them, and re-layouts  84.7 us (4%)
    psum x1, waiting for transfers between devices, per_device(): lax.psum(jnp.einsum('tpc,tdc->pd', grad_pair_low, cross_pair, preferred_e...  204 us
    psum x1, waiting for transfers between devices, per_device(): lax.psum(summed[1].astype(jnp.bfloat16), 'rows').astype(jnp.float32)  116 us
    psum x1, waiting for transfers between devices, per_device(): lax.psum(jnp.dot(self_mixed, self_output, preferred_element_type=jnp.floa...  113 us
    psum x1, waiting for transfers between devices, per_device(): lax.psum(jnp.dot(cross_mixed, cross_output, preferred_element_type=jnp.fl...  85.7 us
    all_gather x8, blocking collectives, owner_key_grads(): lax.all_gather(row_total[:, :, 0].T, 'rows', axis=0, tiled=True)  76.4 us
    all_gather x8, blocking collectives, owner_key_grads(): lax.all_gather(spread[:, :, 0].T, 'rows', axis=0, tiled=True)  74.8 us
    dot_general x16, matrix products, scaled_scores(): jnp.einsum('qhe,khe->hqk', queries, key_rows, preferred_element_type=jnp....  70.2 us
    all_gather x8, waiting for transfers between devices, owner_key_grads(): lax.all_gather(queries, 'rows', axis=0, tiled=True)  69.2 us
  transfers between devices with their start and end apart: 38, of which 23 were waited for; matrix products, arithmetic and copies ran while one was open for 24% of the time, Pallas kernels for 0%

commit v1 on v0

--- a/solution.py
+++ b/solution.py
@@ -6,6 +6,13 @@
 
 HEAD_DIM = 64
 EPSILON = 1e-05
+
+
+def swapped_in(x, mesh_axis, d):
+    devices = lax.axis_size(mesh_axis)
+    blocks = jnp.stack([x for _ in range(devices)])
+    blocks = lax.all_to_all(blocks, mesh_axis, split_axis=0, concat_axis=0)
+    return jnp.concatenate(blocks, axis=d)
 
 
 def layer_norm(inputs):
@@ -94,7 +101,7 @@
         lax.all_gather(grad_mixed, "rows", axis=0, tiled=True),
     )
     gathered_peak, gathered_total, gathered_spread = (
-        lax.all_gather(row_peak[:, :, 0].T, "rows", axis=0, tiled=True),
+        swapped_in(row_peak[:, :, 0].T, "rows", 0),
         lax.all_gather(row_total[:, :, 0].T, "rows", axis=0, tiled=True),
         lax.all_gather(spread[:, :, 0].T, "rows", axis=0, tiled=True),
     )

time: 1920 us -> 1920 us (level)
  blocking collectives: 245 us -> 172 us
  starting transfers between devices: 2.1 us -> 33.5 us
  waiting for transfers between devices: 953 us -> 982 us
    all_gather x8 -> x0, blocking collectives: 68.9 us -> none  [owner_key_grads(): lax.all_gather(row_peak[:, :, 0].T, 'rows', axis=0, tiled=True)]
    all_gather x4, waiting for transfers between devices: 32.6 us -> 65.5 us  [per_device(): lax.all_gather(own_values, 'rows', axis=0, tiled=True)]
    all_to_all x0 -> x8, starting transfers between devices: none -> 31.4 us  [swapped_in(): blocks = lax.all_to_all(blocks, mesh_axis, split_axis=0, concat_axis=0)]
    all_gather x8, waiting for transfers between devices: 69.2 us -> 44.9 us  [owner_key_grads(): lax.all_gather(queries, 'rows', axis=0, tiled=True)]
    unnamed x673 -> x663, local copies, waits for them, and re-layouts: 42.7 us -> 43.2 us
  transfers between devices with their start and end apart: 38 -> 46, of which waited for: 23 -> 25; matrix products, arithmetic and copies ran while one was open for 24% -> 25% of each run, Pallas kernels for 0% -> 0%
where the time goes in v1:
time: 1920 us; the launch traced here: 1910 us
  waiting for transfers between devices  982 us (51%)
  matrix products  491 us (26%)
  blocking collectives  172 us (9%)
  other arithmetic  125 us (7%)
  local copies, waits for them, and re-layouts  90 us (5%)
  starting transfers between devices  33.5 us (2%)
    psum x1, waiting for transfers between devices, per_device(): lax.psum(jnp.einsum('tpc,tdc->pd', grad_pair_low, cross_pair, preferred_e...  204 us
    psum x1, waiting for transfers between devices, per_device(): lax.psum(jnp.dot(self_mixed, self_output, preferred_element_type=jnp.floa...  128 us
    psum x1, waiting for transfers between devices, per_device(): lax.psum(summed[1].astype(jnp.bfloat16), 'rows').astype(jnp.float32)  116 us
    psum x1, waiting for transfers between devices, per_device(): lax.psum(jnp.dot(cross_mixed, cross_output, preferred_element_type=jnp.fl...  85.6 us
    all_gather x8, blocking collectives, owner_key_grads(): lax.all_gather(spread[:, :, 0].T, 'rows', axis=0, tiled=True)  75.1 us
    dot_general x16, matrix products, scaled_scores(): jnp.einsum('qhe,khe->hqk', queries, key_rows, preferred_element_type=jnp....  73.1 us
    all_gather x8, blocking collectives, owner_key_grads(): lax.all_gather(row_total[:, :, 0].T, 'rows', axis=0, tiled=True)  71.9 us
    psum x1, waiting for transfers between devices, per_device(): lax.psum(jnp.einsum('rf,df->rd', grad_pre, widen_weights, preferred_eleme...  68.7 us
  transfers between devices with their start and end apart: 46, of which 25 were waited for; matrix products, arithmetic and copies ran while one was open for 25% of the time, Pallas kernels for 0%

profile of v1, /device:TPU:0, one launch (start us, length us, event | category | flops | bytes accessed | tf_op | source)
XLA Modules:
  0.0 1912.8 jit_solution(11885370948672284006)
XLA Ops:
  36.8 9.3 all-gather.87.cloned.1.call-done
  54.1 17.5 all-gather.85.cloned.1.call-done
  78.5 19.1 all-gather.103.cloned.1.call-done
  105.2 17.8 all-gather.101.cloned.1.call-done
  128.6 20.3 %all-gather.95.cloned.1.call-done = bf16[1,2048,256]{1,2,0:T(8,128)(2,1)} async-done(((bf16[1,256,256]{1,2,0:T(8,128)(2,1)}), bf16[1,2048,256]{1,2,0:T(8,128)(2,1)}) %all-gather.95.cloned.1.call-update) | async-done | bytes 1048592 | tf_op jit(solution)/shard_map/all_gather | solution.py:176
  156.4 17.9 all-gather.93.cloned.1.call-done
  179.9 19.8 %all-gather.79.cloned.1.call-done = bf16[1,2048,256]{1,2,0:T(8,128)(2,1)} async-done(((bf16[1,256,256]{1,2,0:T(8,128)(2,1)}), bf16[1,2048,256]{1,2,0:T(8,128)(2,1)}) %all-gather.79.cloned.1.call-update) | async-done | bytes 1048592 | tf_op jit(solution)/shard_map/all_gather | solution.py:176
  210.0 15.2 all-gather.77.cloned.1.call-done
  265.8 9.5 all_gather.169
  333.6 128.3 %all-reduce.22.cloned.1.call-done = (f32[256,1024]{1,0:T(8,128)}, f32[256,1024]{1,0:T(8,128)}, f32[256,1024]{1,0:T(8,128)}, f32[256,1024]{1,0:T(8,128)}) async-done(((f32[256,1024]{1,0:T(8,128)}, f32[256,1024]{1,0:T(8,128)}, f32[256,1024]{1,0:T(8,128)}, f32[256,1024]{1,0:T(8,128)}), (f32[256,1024]{1,0:T(8,128)}, f32[256,1024]{1,0:T(8,128)}, f32[256,1024]{1,0:T(8,128)}, ...) | async-done | bytes 4194320 | tf_op jit(solution)/shard_map/psum | solution.py:182
  468.0 18.4 all-gather.115.cloned.1.call-done
  494.1 17.9 all-gather.107.cloned.1.call-done
  546.0 17.3 all-gather.89.cloned.1.call-done
  570.9 17.8 all-gather.83.cloned.1.call-done
  596.4 17.8 all-gather.81.cloned.1.call-done
  625.9 14.0 all-gather.105.cloned.1.call-done
  645.7 19.6 %all-gather.99.cloned.1.call-done = bf16[1,2048,256]{1,2,0:T(8,128)(2,1)} async-done(((bf16[1,256,256]{1,2,0:T(8,128)(2,1)}), bf16[1,2048,256]{1,2,0:T(8,128)(2,1)}) %all-gather.99.cloned.1.call-update) | async-done | bytes 1048592 | tf_op jit(solution)/shard_map/all_gather | solution.py:200
  674.4 16.5 all-gather.97.cloned.1.call-done
  698.6 10.0 all_gather.189
  774.5 19.4 %all-gather.61.cloned.1.call-done = bf16[2048,256]{0,1:T(8,128)(2,1)} async-done(((bf16[256,256]{0,1:T(8,128)(2,1)}), bf16[2048,256]{0,1:T(8,128)(2,1)}) %all-gather.61.cloned.1.call-update) | async-done | bytes 1048592 | tf_op jit(solution)/shard_map/all_gather | solution.py:100
  800.2 85.6 %all-reduce.32.cloned.1.call-done = (bf16[256,1024]{1,0:T(8,128)(2,1)}, bf16[256,1024]{1,0:T(8,128)(2,1)}, bf16[256,1024]{1,0:T(8,128)(2,1)}, bf16[256,1024]{1,0:T(8,128)(2,1)}) async-done(((bf16[256,1024]{1,0:T(8,128)(2,1)}, bf16[256,1024]{1,0:T(8,128)(2,1)}, bf16[256,1024]{1,0:T(8,128)(2,1)}, bf16[256,1024]{1,0:T(8,128)(2,1)}), (bf16[256,1024]{1,0:T(8,128)(2,1)}, bf16[256,1024]{1,0:T(8,128)(2,1)}, ...) | async-done | bytes 2097168 | tf_op jit(solution)/shard_map/psum | solution.py:207
  940.6 68.7 %all-reduce.30.cloned.1.call-done = (bf16[256,1024]{1,0:T(8,128)(2,1)}, bf16[256,1024]{1,0:T(8,128)(2,1)}, bf16[256,1024]{1,0:T(8,128)(2,1)}, bf16[256,1024]{1,0:T(8,128)(2,1)}) async-done(((bf16[256,1024]{1,0:T(8,128)(2,1)}, bf16[256,1024]{1,0:T(8,128)(2,1)}, bf16[256,1024]{1,0:T(8,128)(2,1)}, bf16[256,1024]{1,0:T(8,128)(2,1)}), (bf16[256,1024]{1,0:T(8,128)(2,1)}, bf16[256,1024]{1,0:T(8,128)(2,1)}, ...) | async-done | bytes 2097168 | tf_op jit(solution)/shard_map/psum | solution.py:238
  1179.6 61.5 %all-reduce.28.cloned.1.call-done = (bf16[256,1024]{1,0:T(8,128)(2,1)}, bf16[256,1024]{1,0:T(8,128)(2,1)}, bf16[256,1024]{1,0:T(8,128)(2,1)}, bf16[256,1024]{1,0:T(8,128)(2,1)}) async-done(((bf16[256,1024]{1,0:T(8,128)(2,1)}, bf16[256,1024]{1,0:T(8,128)(2,1)}, bf16[256,1024]{1,0:T(8,128)(2,1)}, bf16[256,1024]{1,0:T(8,128)(2,1)}), (bf16[256,1024]{1,0:T(8,128)(2,1)}, bf16[256,1024]{1,0:T(8,128)(2,1)}, ...) | async-done | bytes 2097168 | tf_op jit(solution)/shard_map/psum | solution.py:282
  1272.6 10.3 multiply_reduce_fusion.4
  1293.4 9.2 fusion.176
  1336.0 10.7 all_gather.171
  1346.7 9.3 all_gather.167
  1356.0 10.2 all_gather.163
  1366.2 9.3 all_gather.175
  1471.3 203.8 %all-reduce.26.cloned.1.call-done = (bf16[256,1024]{1,0:T(8,128)(2,1)}, bf16[256,1024]{1,0:T(8,128)(2,1)}, bf16[256,1024]{1,0:T(8,128)(2,1)}, bf16[256,1024]{1,0...) async-done(((bf16[256,1024]{1,0:T(8,128)(2,1)}, ...) | async-done | bytes 6291472 | tf_op jit(solution)/shard_map/psum | solution.py:288
  1722.4 24.8 %all-reduce.9 = (bf16[32,2,256]{2,1,0:T(2,128)(2,1)S(1)}, bf16[256]{0:T(256)(128)(2,1)S(1)}, bf16[256]{0:T(256)(128)(2,1)S(1)}) all-reduce(bf16[32,2,256]{2,1,0:T(2,128)(2,1)S(1)} %dynamic-slice_convert_fusion, bf16[256]{0:T(256)(128)(2,1)S(1)} %dynamic_slice.40, ...), channel_id=1, replica_groups=mesh['heads'=4,'rows'=8] {'rows'}, use_global_device_ids=true, to_apply=%region_100.101 | all-reduce | flops 16896 | bytes 67584 | tf_op jit(solution)/shard_map/psum | solution.py:368
  1769.3 116.2 %all-reduce.24.cloned.1.call-done = (bf16[3,1024,256]{1,2,0:T(8,128)(2,1)}, bf16[2,1024,256]{1,2,0:T(8,128)(2,1)}, bf16[768,256]{0,1:T(8,128)(2,1)}, bf16[256,10...) async-done(((bf16[3,1024,256]{1,2,0:T(8,128)(2,1)}, ...) | async-done | bytes 8781840 | tf_op jit(solution)/shard_map/psum | solution.py:369
  (1108 shorter events, 830.6 us)
Async XLA Ops:
  26.9 147.3 %all-gather.93.cloned.1.call-start = ((), (), s32[]{:S(2)}) async-start(), calls=%async_computation.28 | async-start | bytes 1179648 | tf_op jit(solution)/shard_map/all_gather | solution.py:177
  27.5 172.2 %all-gather.79.cloned.1.call-start = ((), (), s32[]{:S(2)}) async-start(), calls=%async_computation.21 | async-start | bytes 1179648 | tf_op jit(solution)/shard_map/all_gather | solution.py:176
  33.9 191.3 %all-gather.77.cloned.1.call-start = ((), (), s32[]{:S(2)}) async-start(), calls=%async_computation.20 | async-start | bytes 1179648 | tf_op jit(solution)/shard_map/all_gather | solution.py:177
  34.7 270.8 %all-gather.113.cloned.1.call-start = ((), (), s32[]{:S(2)}) async-start(), calls=%async_computation.38 | async-start | bytes 1179648 | tf_op jit(solution)/shard_map/all_gather | solution.py:100
  35.4 281.1 %all-gather.111.cloned.1.call-start = ((), (), s32[]{:S(2)}) async-start(), calls=%async_computation.37 | async-start | bytes 1179648 | tf_op jit(solution)/shard_map/all_gather | solution.py:100
  36.0 291.6 %all-gather.109.cloned.1.call-start = ((), (), s32[]{:S(2)}) async-start(), calls=%async_computation.36 | async-start | bytes 1179648 | tf_op jit(solution)/shard_map/all_gather | solution.py:100
  36.7 425.2 %all-reduce.22.cloned.1.call-start = ((), (), s32[]{:S(2)}) async-start(), calls=%async_computation.40 | async-start | bytes 8388608 | tf_op jit(solution)/shard_map/psum | solution.py:182
  232.8 253.7 %all-gather.115.cloned.1.call-start = ((), (), s32[]{:S(2)}) async-start(), calls=%async_computation.39 | async-start | bytes 1179648 | tf_op jit(solution)/shard_map/all_gather | solution.py:100
  233.6 278.4 %all-gather.107.cloned.1.call-start = ((), (), s32[]{:S(2)}) async-start(), calls=%async_computation.35 | async-start | bytes 1179648 | tf_op jit(solution)/shard_map/all_gather | solution.py:200
  237.9 299.8 %all-gather.91.cloned.1.call-start = ((), (), s32[]{:S(2)}) async-start(), calls=%async_computation.27 | async-start | bytes 1179648 | tf_op jit(solution)/shard_map/all_gather | solution.py:200
  242.2 321.0 %all-gather.89.cloned.1.call-start = ((), (), s32[]{:S(2)}) async-start(), calls=%async_computation.26 | async-start | bytes 1179648 | tf_op jit(solution)/shard_map/all_gather | solution.py:201
  242.8 345.9 %all-gather.83.cloned.1.call-start = ((), (), s32[]{:S(2)}) async-start(), calls=%async_computation.23 | async-start | bytes 1179648 | tf_op jit(solution)/shard_map/all_gather | solution.py:200
  247.0 367.2 %all-gather.81.cloned.1.call-start = ((), (), s32[]{:S(2)}) async-start(), calls=%async_computation.22 | async-start | bytes 1179648 | tf_op jit(solution)/shard_map/all_gather | solution.py:201
  247.6 392.2 %all-gather.105.cloned.1.call-start = ((), (), s32[]{:S(2)}) async-start(), calls=%async_computation.34 | async-start | bytes 1179648 | tf_op jit(solution)/shard_map/all_gather | solution.py:201
  248.4 417.0 %all-gather.99.cloned.1.call-start = ((), (), s32[]{:S(2)}) async-start(), calls=%async_computation.31 | async-start | bytes 1179648 | tf_op jit(solution)/shard_map/all_gather | solution.py:200
  252.1 438.8 %all-gather.97.cloned.1.call-start = ((), (), s32[]{:S(2)}) async-start(), calls=%async_computation.30 | async-start | bytes 1179648 | tf_op jit(solution)/shard_map/all_gather | solution.py:201
  323.4 163.1 %all-to-all-start.3 = ((f32[8,256,4]{1,2,0:T(4,128)}), f32[8,256,4]{1,2,0:T(4,128)S(1)}, u32[]{:S(2)}, u32[]{:S(2)}) async-start(f32[8,256,4]{1,2,0:T(4,128)} %stack.84), calls=%async_computation.3 | async-start | bytes 65536 | tf_op jit(solution)/shard_map/all_to_all | solution.py:14
  327.6 411.9 %all-gather.73.cloned.1.call-start = ((), (), s32[]{:S(2)}) async-start(), calls=%async_computation.18 | async-start | bytes 1179648 | tf_op jit(solution)/shard_map/all_gather | solution.py:100
  468.0 282.4 %all-gather.69.cloned.1.call-start = ((), (), s32[]{:S(2)}) async-start(), calls=%async_computation.16 | async-start | bytes 1179648 | tf_op jit(solution)/shard_map/all_gather | solution.py:100
  518.4 216.5 %all-to-all-start.7 = ((f32[8,256,4]{1,2,0:T(4,128)}), f32[8,256,4]{1,2,0:T(4,128)}, u32[]{:S(2)}, u32[]{:S(2)}) async-start(f32[8,256,4]{1,2,0:T(4,128)} %stack.192), calls=%async_computation.7 | async-start | bytes 65536 | tf_op jit(solution)/shard_map/all_to_all | solution.py:14
  522.3 246.0 %all-gather.65.cloned.1.call-start = ((), (), s32[]{:S(2)}) async-start(), calls=%async_computation.14 | async-start | bytes 1179648 | tf_op jit(solution)/shard_map/all_gather | solution.py:100
  529.8 264.1 %all-gather.61.cloned.1.call-start = ((), (), s32[]{:S(2)}) async-start(), calls=%async_computation.12 | async-start | bytes 1179648 | tf_op jit(solution)/shard_map/all_gather | solution.py:100
  625.8 260.0 %all-reduce.32.cloned.1.call-start = ((), (), s32[]{:S(2)}) async-start(), calls=%async_computation.45 | async-start | bytes 4194304 | tf_op jit(solution)/shard_map/psum | solution.py:207
  761.3 248.0 %all-reduce.30.cloned.1.call-start = ((), (), s32[]{:S(2)}) async-start(), calls=%async_computation.44 | async-start | bytes 4194304 | tf_op jit(solution)/shard_map/psum | solution.py:238
  922.2 200.2 %all-gather.75.cloned.1.call-start = ((), (), s32[]{:S(2)}) async-start(), calls=%async_computation.19 | async-start | bytes 1179648 | tf_op jit(solution)/shard_map/all_gather | solution.py:101
  1111.9 129.2 %all-reduce.28.cloned.1.call-start = ((), (), s32[]{:S(2)}) async-start(), calls=%async_computation.43 | async-start | bytes 4194304 | tf_op jit(solution)/shard_map/psum | solution.py:282
  1122.3 253.7 %all-gather.57.cloned.1.call-start = ((), (), s32[]{:S(2)}) async-start(), calls=%async_computation.10 | async-start | bytes 1179648 | tf_op jit(solution)/shard_map/all_gather | solution.py:101
  1258.5 133.1 %all-gather.55.cloned.1.call-start = ((), (), s32[]{:S(2)}) async-start(), calls=%async_computation.9 | async-start | bytes 1179648 | tf_op jit(solution)/shard_map/all_gather | solution.py:101
  1272.5 134.8 %all-gather.53.cloned.1.call-start = ((), (), s32[]{:S(2)}) async-start(), calls=%async_computation.8 | async-start | bytes 1179648 | tf_op jit(solution)/shard_map/all_gather | solution.py:101
  1291.3 131.6 %all-gather.59.cloned.1.call-start = ((), (), s32[]{:S(2)}) async-start(), calls=%async_computation.11 | async-start | bytes 1179648 | tf_op jit(solution)/shard_map/all_gather | solution.py:101
  1375.6 299.5 %all-reduce.26.cloned.1.call-start = ((), (), s32[]{:S(2)}) async-start(), calls=%async_computation.42 | async-start | bytes 12582912 | tf_op jit(solution)/shard_map/psum | solution.py:288
  1449.4 436.1 %all-reduce.24.cloned.1.call-start = ((), (), s32[]{:S(2)}) async-start(), calls=%async_computation.41 | async-start | bytes 17563648 | tf_op jit(solution)/shard_map/psum | solution.py:369
  (344 other events, 12312.5 us)
Sparse Core Ops, SparseCore 0:
  19.8 26.2 all-gather.86
  47.9 23.5 all-gather.84
  74.0 23.5 all-gather.102
  99.4 23.5 all-gather.100
  125.3 23.5 all-gather.94
  150.6 23.5 all-gather.92
  176.1 23.5 all-gather.78
  201.6 23.5 all-gather.76
  253.0 23.6 all-gather.110
  278.5 23.6 all-gather.108
  305.9 156.0 all-reduce.21
  488.4 23.5 all-gather.106
  513.9 23.8 all-gather.90
  539.6 23.5 all-gather.88
  565.1 23.5 all-gather.82
  590.6 23.5 all-gather.80
  616.2 23.5 all-gather.104
  641.7 23.5 all-gather.98
  667.4 23.5 all-gather.96
  693.0 23.7 all-gather.72
  718.8 23.6 all-gather.68
  744.3 23.9 all-gather.64
  770.3 23.5 all-gather.60
  797.7 88.0 all-reduce.31
  922.3 86.9 all-reduce.29
  1100.3 23.6 all-gather.66
  1126.6 23.6 all-gather.62
  1153.0 88.0 all-reduce.27
  1283.1 23.5 all-gather.54
  1309.1 23.6 all-gather.52
  1449.5 225.5 all-reduce.25
  1755.1 130.3 all-reduce.23
  (6 shorter events, 134.4 us)
